TPU v7x, 256 devices: a whole 4x4x8 slice. The times are simulated.
256 devices in a mesh: row: 4 (over x), col: 16 (over y, z_lo), gz: 4 (over z_hi, core).
Axes of the slice: x: 4, y: 4, z: 8 (z_hi: 2, z_lo: 4; z = z_hi * 4 + z_lo), core: 2. Of those that a mesh axis runs over, the one named last changes fastest.
Arguments:
- volume_field: bfloat16 [128, 32, 128, 512], P(None, 'row', 'col', 'gz'), may hold values from -6 to 6
- volume_load: bfloat16 [128, 32, 128, 512], P(None, 'row', 'col', 'gz'), may hold values from -6 to 6
- coefficient: float32 [32, 128, 512], P('row', 'col', 'gz'), may hold values from 0.25 to 2
- surface_block: bfloat16 [1024, 262144], P('row', 'col'), may hold values from -0.015625 to 0.015625
- trace_cell: int32 [4, 16, 4, 1024], P('row', 'col', 'gz'), may hold values from 0 to 8191, as said below
- flux_cell: int32 [4, 16, 4, 4], P('row', 'col', 'gz'), may hold values from 0 to 8191, as said below
Outputs:
- new_field: bfloat16 [128, 32, 128, 512], P(None, 'row', 'col', 'gz')
- surface_flux: float32 [128, 1024], P('gz', ('row', 'col'))
Inputs may be any that keep to these rules, and one draw needn't show every extreme that they name: `trace_cell`: within each device's 1024 entries, entry values are local cell numbers, one from each aligned run of 8 consecutive cells, in a permuted order; the first and last cells of the block are always chosen. `flux_cell`: within each device's 4 entries, entry values are local cell numbers, one from each aligned run of 2048 consecutive cells, in a permuted order; the first and last cells of the block are always chosen.
All inputs are finite; a program needn't handle non-finite values.
Results may differ from a plain program's by a relative error of at most 0.0032.
Values may be sent and summed in bfloat16 or wider, within the bound.
A program may use at most 128 MiB of HBM per device.

v0:
```python
import jax
import jax.numpy as jnp
from jax import lax
from jax.sharding import PartitionSpec as P

OMEGA = 0.8


def padded_2(array, sides, width):
    for axis, dim in sides:
        peers, length = (lax.axis_size(axis), array.shape[dim])
        up = [(i, (i + 1) % peers) for i in range(peers - 1)]
        down = [(j, i) for i, j in up]
        last = lax.slice_in_dim(array, length - width, length, axis=dim)
        first = lax.slice_in_dim(array, 0, width, axis=dim)
        before = lax.ppermute(last, axis, up)
        after = lax.ppermute(first, axis, down)
        array = jnp.concatenate([before, array, after], axis=dim)
    return array


def relax(current, source, diagonal):
    padded = padded_2(current, (("row", 1), ("col", 2), ("gz", 3)), 1).astype(jnp.float32)
    centre = current.astype(jnp.float32)
    beside = padded[:, 2:, 1:-1, 1:-1] + padded[:, :-2, 1:-1, 1:-1]
    beside = beside + padded[:, 1:-1, 2:, 1:-1] + padded[:, 1:-1, :-2, 1:-1]
    beside = beside + padded[:, 1:-1, 1:-1, 2:] + padded[:, 1:-1, 1:-1, :-2]
    return (centre + OMEGA * (source - (diagonal * centre - beside)) / diagonal).astype(
        jnp.bfloat16
    )


def per_device(volume_field, volume_load, coefficient, surface_block, trace_cell, flux_cell):
    side_count, first_span, second_span, third_span = volume_field.shape
    cell_count = first_span * second_span * third_span
    slot_count = trace_cell.shape[3]
    flux_slots = flux_cell.shape[3]
    side_group = side_count // lax.axis_size("gz")
    flat_field = volume_field.reshape(side_count, cell_count)
    picker = (
        lax.broadcasted_iota(jnp.int32, (cell_count, slot_count), 0)
        == trace_cell.reshape(1, slot_count)
    ).astype(jnp.bfloat16)
    trace_values = jnp.dot(flat_field, picker, preferred_element_type=jnp.float32).astype(
        jnp.bfloat16
    )
    layer_index = lax.axis_index("gz")
    chosen = lax.dynamic_slice_in_dim(
        lax.all_gather(trace_values, ("row", "gz"), axis=1, tiled=True),
        layer_index * side_group,
        side_group,
        0,
    )
    partial_flux = lax.dot_general(
        chosen, surface_block, (((1,), (1,)), ((), ())), preferred_element_type=jnp.float32
    )
    surface_flux = lax.psum_scatter(partial_flux, "col", scatter_dimension=1, tiled=True)
    owned_flux = lax.all_to_all(surface_flux, "gz", split_axis=1, concat_axis=0, tiled=True)
    placer = (
        flux_cell.reshape(flux_slots, 1)
        == lax.broadcasted_iota(jnp.int32, (flux_slots, cell_count), 1)
    ).astype(jnp.float32)
    placed = jnp.dot(
        owned_flux, placer, precision=lax.Precision.HIGHEST, preferred_element_type=jnp.float32
    )
    source = volume_load.astype(jnp.float32) + placed.reshape(
        side_count, first_span, second_span, third_span
    )
    diagonal = 6.0 + coefficient
    current = volume_field
    for repeat in range(3):
        current = relax(current, source, diagonal)
    return (current, surface_flux)


def solution(mesh):
    in_specs = (
        P(None, "row", "col", "gz"),
        P(None, "row", "col", "gz"),
        P("row", "col", "gz"),
        P("row", "col"),
        P("row", "col", "gz", None),
        P("row", "col", "gz", None),
    )
    out_specs = (P(None, "row", "col", "gz"), P("gz", ("row", "col")))
    return jax.shard_map(
        per_device, mesh=mesh, in_specs=in_specs, out_specs=out_specs, check_vma=False
    )
```

profile of v0, /device:TPU:17, one launch (start us, length us, event | category | flops | bytes accessed | tf_op | source)
XLA Modules:
  0.0 316.4 jit_solution(1257853080280869536)
XLA Ops:
  7.2 0.0 all-gather.2.cloned.1.call-start
  7.2 8.3 %fusion.22 = bf16[128,1024]{1,0:T(8,128)(2,1)} fusion(bf16[16,8,64,128]{3,2,1,0:T(8,128)(2,1)} %bitcast.27, s32[1024]{0:T(1024)} %bitcast.29), kind=kOutput, calls=%fused_computation.46 | convolution fusion | flops 2156003328 | bytes 2363392 | tf_op jit(solution)/shard_map/dot_general | solution.py:44
  15.5 0.0 all-gather.2.cloned.1.call-update
  15.5 0.0 copy-start.1
  15.6 0.0 reduce-scatter.2.cloned.1.call-start
  15.6 3.3 %copy.15 = bf16[128,8,8,128]{0,3,2,1:T(8,128)(2,1)S(1)} copy(bf16[128,8,8,128]{3,2,1,0:T(8,128)(2,1)} %param.6) | data formatting | bytes 4194304 | tf_op args[0]
  19.0 3.1 collective-permute-start
  22.1 1.3 collective-permute-start.1
  23.4 3.7 %collective-permute-done = bf16[128,1,8,128]{0,3,2,1:T(8,128)(2,1)S(1)} collective-permute-done((bf16[128,1,8,128]{0,3,2,1:T(8,128)(2,1)S(1)}, bf16[128,1,8,128]{0,3,2,1:T(8,128)(2,1)S(1)}, u32[]{:S(2)}, u32[]{:S(2)}) %collective-permute-start) | collective-permute-done | bytes 262176 | tf_op jit(solution)/shard_map/ppermute | solution.py:16
  27.1 3.8 %collective-permute-done.1 = bf16[128,1,8,128]{0,3,2,1:T(8,128)(2,1)S(1)} collective-permute-done((bf16[128,1,8,128]{0,3,2,1:T(8,128)(2,1)S(1)}, bf16[128,1,8,128]{0,3,2,1:T(8,128)(2,1)S(1)}, u32[]{:S(2)}, u32[]{:S(2)}) %collective-permute-start.1) | collective-permute-done | bytes 262176 | tf_op jit(solution)/shard_map/ppermute | solution.py:17
  30.9 0.9 pad_maximum_fusion.8
  31.8 3.5 %collective-permute-start.2 = (bf16[128,10,1,128]{0,3,2,1:T(8,128)(2,1)}, bf16[128,10,1,128]{0,3,2,1:T(8,128)(2,1)S(1)}, u32[]{:S(2)}, u32[]{:S(2)}) collective-permute-start(bf16[128,10,1,128]{0,3,2,1:T(8,128)(2,1)} %get-tuple-element.16), channel_id=1, source_target_pairs={{0,4},{4,8},{8,12},{12,16},{16,20},{20,24},{24,28},{28,32},{32,36}... | collective-permute-start | bytes 983048 | tf_op jit(solution)/shard_map/ppermute | solution.py:16
  35.4 4.5 %collective-permute-start.3 = (bf16[128,10,1,128]{0,3,2,1:T(8,128)(2,1)}, bf16[128,10,1,128]{0,3,2,1:T(8,128)(2,1)S(1)}, u32[]{:S(2)}, u32[]{:S(2)}) collective-permute-start(bf16[128,10,1,128]{0,3,2,1:T(8,128)(2,1)} %get-tuple-element.17), channel_id=1, source_target_pairs={{4,0},{8,4},{12,8},{16,12},{20,16},{24,20},{28,24},{32,28},{36,32}... | collective-permute-start | bytes 983048 | tf_op jit(solution)/shard_map/ppermute | solution.py:17
  39.9 8.5 %collective-permute-done.2 = bf16[128,10,1,128]{0,3,2,1:T(8,128)(2,1)S(1)} collective-permute-done((bf16[128,10,1,128]{0,3,2,1:T(8,128)(2,1)}, bf16[128,10,1,128]{0,3,2,1:T(8,128)(2,1)S(1)}, u32[]{:S(2)}, u32[]{:S(2)}) %collective-permute-start.2) | collective-permute-done | bytes 327712 | tf_op jit(solution)/shard_map/ppermute | solution.py:16
  48.5 5.0 %collective-permute-done.3 = bf16[128,10,1,128]{0,3,2,1:T(8,128)(2,1)S(1)} collective-permute-done((bf16[128,10,1,128]{0,3,2,1:T(8,128)(2,1)}, bf16[128,10,1,128]{0,3,2,1:T(8,128)(2,1)S(1)}, u32[]{:S(2)}, u32[]{:S(2)}) %collective-permute-start.3) | collective-permute-done | bytes 327712 | tf_op jit(solution)/shard_map/ppermute | solution.py:17
  53.5 0.1 pad_maximum_fusion.23
  53.6 8.9 %collective-permute-start.4 = (bf16[128,10,10,1]{0,3,2,1:T(2,128)(2,1)S(1)}, bf16[128,10,10,1]{0,3,2,1:T(2,128)(2,1)S(1)}, u32[]{:S(2)}, u32[]{:S(2)}) collective-permute-start(bf16[128,10,10,1]{0,3,2,1:T(2,128)(2,1)S(1)} %get-tuple-element.10), channel_id=1, source_target_pairs={{0,1},{1,2},{2,3},{4,5},{5,6},{6,7},{8,9},{9,10},{10,11},{12,13},{... | collective-permute-start | bytes 76808 | tf_op jit(solution)/shard_map/ppermute | solution.py:16
  62.5 1.9 collective-permute-start.5
  64.4 32.9 %all-gather.2.cloned.1.call-done = bf16[128,16384]{1,0:T(8,128)(2,1)} async-done(((bf16[128,1024]{1,0:T(8,128)(2,1)}), bf16[128,16384]{1,0:T(8,128)(2,1)}) %all-gather.2.cloned.1.call-update) | async-done | bytes 4194320 | tf_op jit(solution)/shard_map/all_gather | solution.py:49
  97.4 6.7 %fusion.25 = f32[32,256]{0,1:T(8,128)} fusion(bf16[256,16384]{1,0:T(8,128)(2,1)} %param.9, bf16[128,16384]{1,0:T(8,128)(2,1)} %all-gather.2.cloned.1.call-done, s32[]{:T(128)S(6)} %select_n.3), kind=kOutput, calls=%fused_computation.47 | convolution fusion | flops 268435456 | bytes 9469956 | tf_op jit(solution)/shard_map/dot_general | solution.py:54
  104.0 0.0 reduce-scatter.2.cloned.1.call-update
  104.1 4.2 %copy.16 = bf16[128,8,8,128]{0,3,2,1:T(8,128)(2,1)} copy(bf16[128,8,8,128]{3,2,1,0:T(8,128)(2,1)} %param.7) | data formatting | bytes 4194304 | tf_op args[1]
  108.3 53.4 %reduce-scatter.2.cloned.1.call-done = f32[32,16]{0,1:T(8,128)} async-done(((f32[32,256]{0,1:T(8,128)}), f32[32,16]{0,1:T(8,128)}) %reduce-scatter.2.cloned.1.call-update) | async-done | bytes 2064 | tf_op jit(solution)/shard_map/reduce_scatter | solution.py:57
  161.7 1.4 reshape.41
  163.1 17.1 %all-to-all-start = ((f32[4,1,128]{2,1,0:T(1,128)}), f32[4,1,128]{2,1,0:T(1,128)}, u32[]{:S(2)}, u32[]{:S(2)}) async-start(f32[4,1,128]{2,1,0:T(1,128)} %reshape.41), calls=%async_computation.1 | async-start | bytes 4096 | tf_op jit(solution)/shard_map/all_to_all | solution.py:58
  180.1 0.0 collective-permute-done.4
  180.1 4.7 %maximum_convert_fusion = f32[128,10,10,130]{0,3,2,1:T(8,128)} fusion(bf16[128,10,10,1]{0,3,2,1:T(2,128)(2,1)S(1)} %collective-permute-done.5, bf16[128,10,1,128]{0,3,2,1:T(8,128)(2,1)S(1)} %collective-permute-done.3, bf16[128,1,8,128]{0,3,2,1:T(8,128)(2,1)S(1)} %collective-permute-done.1, bf16[128,8,8,128]{0,3,2,1:T(8,128)(2,1)S(1)} %copy.15, ...), kind=kLoop, calls=%fused_computation.40 | loop fusion | flops 23296000 | bytes 9984000 | tf_op jit(solution)/shard_map/convert_element_type | solution.py:23
  184.9 2.0 all-to-all-done
  186.9 0.5 broadcast.32
  187.4 1.2 reduce
  188.6 0.1 reshape.42
  188.7 0.1 reshape.39
  188.8 14.0 %fusion.14 = (bf16[128,8,8,128]{0,3,2,1:T(8,128)(2,1)S(1)}, f32[128,8,8,128]{0,3,2,1:T(8,128)}) fusion(f32[128,10,10,130]{0,3,2,1:T(8,128)} %maximum_convert_fusion, bf16[128,8,8,128]{0,3,2,1:T(8,128)(2,1)S(1)} %copy.15, f32[8,8,128]{2,1,0:T(8,128)S(1)} %broadcast_add_fusion, s32[8,8,128]{2,1,0:T(8,128)S(1)} %multiply_add_fusion, s32[4]{0:T(128)S(1)} %bitcast.30, ...), kind=kOutput, calls=%fused_computation.37 | convolution fusion | flops 66093056 | bytes 35719184 | tf_op jit(solution)/shard_map/dot_general | solution.py:63
  202.8 3.0 collective-permute-start.6
  205.8 1.3 collective-permute-start.7
  207.1 3.3 %collective-permute-done.6 = bf16[128,1,8,128]{0,3,2,1:T(8,128)(2,1)S(1)} collective-permute-done((bf16[128,1,8,128]{0,3,2,1:T(8,128)(2,1)S(1)}, bf16[128,1,8,128]{0,3,2,1:T(8,128)(2,1)S(1)}, u32[]{:S(2)}, u32[]{:S(2)}) %collective-permute-start.6) | collective-permute-done | bytes 262176 | tf_op jit(solution)/shard_map/ppermute | solution.py:16
  210.4 3.8 %collective-permute-done.7 = bf16[128,1,8,128]{0,3,2,1:T(8,128)(2,1)S(1)} collective-permute-done((bf16[128,1,8,128]{0,3,2,1:T(8,128)(2,1)S(1)}, bf16[128,1,8,128]{0,3,2,1:T(8,128)(2,1)S(1)}, u32[]{:S(2)}, u32[]{:S(2)}) %collective-permute-start.7) | collective-permute-done | bytes 262176 | tf_op jit(solution)/shard_map/ppermute | solution.py:17
  214.3 0.1 pad_maximum_fusion.5
  214.4 2.8 collective-permute-start.8
  217.2 5.1 %collective-permute-start.9 = (bf16[128,10,1,128]{0,3,2,1:T(8,128)(2,1)S(1)}, bf16[128,10,1,128]{0,3,2,1:T(8,128)(2,1)S(1)}, u32[]{:S(2)}, u32[]{:S(2)}) collective-permute-start(bf16[128,10,1,128]{0,3,2,1:T(8,128)(2,1)S(1)} %get-tuple-element.15), channel_id=1, source_target_pairs={{4,0},{8,4},{12,8},{16,12},{20,16},{24,20},{28,24},{32,28},{36,32}... | collective-permute-start | bytes 983048 | tf_op jit(solution)/shard_map/ppermute | solution.py:17
  222.4 3.8 %collective-permute-done.8 = bf16[128,10,1,128]{0,3,2,1:T(8,128)(2,1)S(1)} collective-permute-done((bf16[128,10,1,128]{0,3,2,1:T(8,128)(2,1)S(1)}, bf16[128,10,1,128]{0,3,2,1:T(8,128)(2,1)S(1)}, u32[]{:S(2)}, u32[]{:S(2)}) %collective-permute-start.8) | collective-permute-done | bytes 327712 | tf_op jit(solution)/shard_map/ppermute | solution.py:16
  226.1 6.6 %collective-permute-done.9 = bf16[128,10,1,128]{0,3,2,1:T(8,128)(2,1)S(1)} collective-permute-done((bf16[128,10,1,128]{0,3,2,1:T(8,128)(2,1)S(1)}, bf16[128,10,1,128]{0,3,2,1:T(8,128)(2,1)S(1)}, u32[]{:S(2)}, u32[]{:S(2)}) %collective-permute-start.9) | collective-permute-done | bytes 327712 | tf_op jit(solution)/shard_map/ppermute | solution.py:17
  232.7 0.1 pad_maximum_fusion.18
  232.8 9.6 %collective-permute-start.10 = (bf16[128,10,10,1]{0,3,2,1:T(2,128)(2,1)S(1)}, bf16[128,10,10,1]{0,3,2,1:T(2,128)(2,1)S(1)}, u32[]{:S(2)}, u32[]{:S(2)}) collective-permute-start(bf16[128,10,10,1]{0,3,2,1:T(2,128)(2,1)S(1)} %get-tuple-element.8), channel_id=1, source_target_pairs={{0,1},{1,2},{2,3},{4,5},{5,6},{6,7},{8,9},{9,10},{10,11},{12,13},{... | collective-permute-start | bytes 76808 | tf_op jit(solution)/shard_map/ppermute | solution.py:16
  242.5 2.2 collective-permute-start.11
  244.7 7.4 %collective-permute-done.11 = bf16[128,10,10,1]{0,3,2,1:T(2,128)(2,1)S(1)} collective-permute-done((bf16[128,10,10,1]{0,3,2,1:T(2,128)(2,1)S(1)}, bf16[128,10,10,1]{0,3,2,1:T(2,128)(2,1)S(1)}, u32[]{:S(2)}, u32[]{:S(2)}) %collective-permute-start.11) | collective-permute-done | bytes 25632 | tf_op jit(solution)/shard_map/ppermute | solution.py:17
  252.1 3.0 maximum_convert_fusion.1
  255.1 4.5 %fusion.15 = bf16[128,8,8,128]{0,3,2,1:T(8,128)(2,1)S(1)} fusion(f32[128,8,8,128]{0,3,2,1:T(8,128)S(1)} %copy-done, f32[128,10,10,130]{0,3,2,1:T(8,128)S(1)} %maximum_convert_fusion.1, bf16[128,8,8,128]{0,3,2,1:T(8,128)(2,1)S(1)} %get-tuple-element.24, f32[8,8,128]{2,1,0:T(8,128)S(1)} %broadcast_add_fusion), kind=kLoop, calls=%fused_computation.38 | loop fusion | flops 13631488 | bytes 33587200 | tf_op jit(solution)/shard_map/convert_element_type | solution.py:28
  259.7 3.1 collective-permute-start.12
  262.8 1.3 collective-permute-start.13
  264.1 2.0 collective-permute-done.12
  266.0 3.8 %collective-permute-done.13 = bf16[128,1,8,128]{0,3,2,1:T(8,128)(2,1)S(1)} collective-permute-done((bf16[128,1,8,128]{0,3,2,1:T(8,128)(2,1)S(1)}, bf16[128,1,8,128]{0,3,2,1:T(8,128)(2,1)S(1)}, u32[]{:S(2)}, u32[]{:S(2)}) %collective-permute-start.13) | collective-permute-done | bytes 262176 | tf_op jit(solution)/shard_map/ppermute | solution.py:17
  269.9 0.1 pad_maximum_fusion.2
  270.0 4.6 %collective-permute-start.14 = (bf16[128,10,1,128]{0,3,2,1:T(8,128)(2,1)S(1)}, bf16[128,10,1,128]{0,3,2,1:T(8,128)(2,1)S(1)}, u32[]{:S(2)}, u32[]{:S(2)}) collective-permute-start(bf16[128,10,1,128]{0,3,2,1:T(8,128)(2,1)S(1)} %get-tuple-element.12), channel_id=1, source_target_pairs={{0,4},{4,8},{8,12},{12,16},{16,20},{20,24},{24,28},{28,32},{32,36}... | collective-permute-start | bytes 983048 | tf_op jit(solution)/shard_map/ppermute | solution.py:16
  274.5 3.4 %collective-permute-start.15 = (bf16[128,10,1,128]{0,3,2,1:T(8,128)(2,1)S(1)}, bf16[128,10,1,128]{0,3,2,1:T(8,128)(2,1)S(1)}, u32[]{:S(2)}, u32[]{:S(2)}) collective-permute-start(bf16[128,10,1,128]{0,3,2,1:T(8,128)(2,1)S(1)} %get-tuple-element.13), channel_id=1, source_target_pairs={{4,0},{8,4},{12,8},{16,12},{20,16},{24,20},{28,24},{32,28},{36,32}... | collective-permute-start | bytes 983048 | tf_op jit(solution)/shard_map/ppermute | solution.py:17
  278.0 5.4 %collective-permute-done.14 = bf16[128,10,1,128]{0,3,2,1:T(8,128)(2,1)S(1)} collective-permute-done((bf16[128,10,1,128]{0,3,2,1:T(8,128)(2,1)S(1)}, bf16[128,10,1,128]{0,3,2,1:T(8,128)(2,1)S(1)}, u32[]{:S(2)}, u32[]{:S(2)}) %collective-permute-start.14) | collective-permute-done | bytes 327712 | tf_op jit(solution)/shard_map/ppermute | solution.py:16
  283.3 4.6 %collective-permute-done.15 = bf16[128,10,1,128]{0,3,2,1:T(8,128)(2,1)S(1)} collective-permute-done((bf16[128,10,1,128]{0,3,2,1:T(8,128)(2,1)S(1)}, bf16[128,10,1,128]{0,3,2,1:T(8,128)(2,1)S(1)}, u32[]{:S(2)}, u32[]{:S(2)}) %collective-permute-start.15) | collective-permute-done | bytes 327712 | tf_op jit(solution)/shard_map/ppermute | solution.py:17
  287.9 0.1 pad_maximum_fusion.13
  288.0 1.9 collective-permute-start.16
  289.9 2.4 collective-permute-start.17
  292.3 6.9 %collective-permute-done.17 = bf16[128,10,10,1]{0,3,2,1:T(2,128)(2,1)S(1)} collective-permute-done((bf16[128,10,10,1]{0,3,2,1:T(2,128)(2,1)S(1)}, bf16[128,10,10,1]{0,3,2,1:T(2,128)(2,1)S(1)}, u32[]{:S(2)}, u32[]{:S(2)}) %collective-permute-start.17) | collective-permute-done | bytes 25632 | tf_op jit(solution)/shard_map/ppermute | solution.py:17
  299.3 3.0 maximum_convert_fusion.2
  302.2 4.5 %fusion.16 = bf16[128,8,8,128]{0,3,2,1:T(8,128)(2,1)S(1)} fusion(f32[128,8,8,128]{0,3,2,1:T(8,128)S(1)} %copy-done, f32[128,10,10,130]{0,3,2,1:T(8,128)S(1)} %maximum_convert_fusion.2, bf16[128,8,8,128]{0,3,2,1:T(8,128)(2,1)S(1)} %fusion.15, f32[8,8,128]{2,1,0:T(8,128)S(1)} %broadcast_add_fusion), kind=kLoop, calls=%fused_computation.39 | loop fusion | flops 13631488 | bytes 33587200 | tf_op jit(solution)/shard_map/convert_element_type | solution.py:28
  306.8 2.8 copy.21
  (15 shorter events, 0.2 us)
Async XLA Ops:
  7.2 90.2 %all-gather.2.cloned.1.call-start = ((), (), s32[]{:S(2)}) async-start(), calls=%async_computation.2 | async-start | bytes 4456448 | tf_op jit(solution)/shard_map/all_gather | solution.py:49
  15.5 24.4 %copy-start.1 = (f32[8,8,128]{2,1,0:T(8,128)S(1)}, f32[8,8,128]{2,1,0:T(8,128)}, u32[]{:S(2)}) copy-start(f32[8,8,128]{2,1,0:T(8,128)} %param.8) | copy-start | bytes 98308
  15.6 146.1 %reduce-scatter.2.cloned.1.call-start = ((), (), s32[]{:S(2)}) async-start(), calls=%async_computation.3 | async-start | bytes 139264 | tf_op jit(solution)/shard_map/reduce_scatter | solution.py:57
  19.0 8.1 %collective-permute-start = (bf16[128,1,8,128]{0,3,2,1:T(8,128)(2,1)S(1)}, bf16[128,1,8,128]{0,3,2,1:T(8,128)(2,1)S(1)}, u32[]{:S(2)}, u32[]{:S(2)}) collective-permute-start(bf16[128,1,8,128]{0,3,2,1:T(8,128)(2,1)S(1)} %get-tuple-element.22), channel_id=1, source_target_pairs={{0,64},{64,128},{128,192},{1,65},{65,129},{129,193},{2,66},{66,130... | collective-permute-start | bytes 786440 | tf_op jit(solution)/shard_map/ppermute | solution.py:16
  22.1 8.8 %collective-permute-start.1 = (bf16[128,1,8,128]{0,3,2,1:T(8,128)(2,1)S(1)}, bf16[128,1,8,128]{0,3,2,1:T(8,128)(2,1)S(1)}, u32[]{:S(2)}, u32[]{:S(2)}) collective-permute-start(bf16[128,1,8,128]{0,3,2,1:T(8,128)(2,1)S(1)} %get-tuple-element.23), channel_id=1, source_target_pairs={{64,0},{128,64},{192,128},{65,1},{129,65},{193,129},{66,2},{130,66... | collective-permute-start | bytes 786440 | tf_op jit(solution)/shard_map/ppermute | solution.py:17
  31.8 16.6 %collective-permute-start.2 = (bf16[128,10,1,128]{0,3,2,1:T(8,128)(2,1)}, bf16[128,10,1,128]{0,3,2,1:T(8,128)(2,1)S(1)}, u32[]{:S(2)}, u32[]{:S(2)}) collective-permute-start(bf16[128,10,1,128]{0,3,2,1:T(8,128)(2,1)} %get-tuple-element.16), channel_id=1, source_target_pairs={{0,4},{4,8},{8,12},{12,16},{16,20},{20,24},{24,28},{28,32},{32,36}... | collective-permute-start | bytes 983048 | tf_op jit(solution)/shard_map/ppermute | solution.py:16
  35.4 18.1 %collective-permute-start.3 = (bf16[128,10,1,128]{0,3,2,1:T(8,128)(2,1)}, bf16[128,10,1,128]{0,3,2,1:T(8,128)(2,1)S(1)}, u32[]{:S(2)}, u32[]{:S(2)}) collective-permute-start(bf16[128,10,1,128]{0,3,2,1:T(8,128)(2,1)} %get-tuple-element.17), channel_id=1, source_target_pairs={{4,0},{8,4},{12,8},{16,12},{20,16},{24,20},{28,24},{32,28},{36,32}... | collective-permute-start | bytes 983048 | tf_op jit(solution)/shard_map/ppermute | solution.py:17
  53.6 126.6 %collective-permute-start.4 = (bf16[128,10,10,1]{0,3,2,1:T(2,128)(2,1)S(1)}, bf16[128,10,10,1]{0,3,2,1:T(2,128)(2,1)S(1)}, u32[]{:S(2)}, u32[]{:S(2)}) collective-permute-start(bf16[128,10,10,1]{0,3,2,1:T(2,128)(2,1)S(1)} %get-tuple-element.10), channel_id=1, source_target_pairs={{0,1},{1,2},{2,3},{4,5},{5,6},{6,7},{8,9},{9,10},{10,11},{12,13},{... | collective-permute-start | bytes 76808 | tf_op jit(solution)/shard_map/ppermute | solution.py:16
  62.5 117.6 %collective-permute-start.5 = (bf16[128,10,10,1]{0,3,2,1:T(2,128)(2,1)S(1)}, bf16[128,10,10,1]{0,3,2,1:T(2,128)(2,1)S(1)}, u32[]{:S(2)}, u32[]{:S(2)}) collective-permute-start(bf16[128,10,10,1]{0,3,2,1:T(2,128)(2,1)S(1)} %get-tuple-element.11), channel_id=1, source_target_pairs={{1,0},{2,1},{3,2},{5,4},{6,5},{7,6},{9,8},{10,9},{11,10},{13,12},{... | collective-permute-start | bytes 76808 | tf_op jit(solution)/shard_map/ppermute | solution.py:17
  163.1 23.9 %all-to-all-start = ((f32[4,1,128]{2,1,0:T(1,128)}), f32[4,1,128]{2,1,0:T(1,128)}, u32[]{:S(2)}, u32[]{:S(2)}) async-start(f32[4,1,128]{2,1,0:T(1,128)} %reshape.41), calls=%async_computation.1 | async-start | bytes 4096 | tf_op jit(solution)/shard_map/all_to_all | solution.py:58
  180.1 8.7 %copy-start.2 = (s32[1,1,1,4]{3,2,1,0:T(1,128)S(1)}, s32[1,1,1,4]{3,2,1,0:T(1,128)}, u32[]{:S(2)}) copy-start(s32[1,1,1,4]{3,2,1,0:T(1,128)} %param.11) | copy-start | bytes 52
  202.8 7.6 %collective-permute-start.6 = (bf16[128,1,8,128]{0,3,2,1:T(8,128)(2,1)S(1)}, bf16[128,1,8,128]{0,3,2,1:T(8,128)(2,1)S(1)}, u32[]{:S(2)}, u32[]{:S(2)}) collective-permute-start(bf16[128,1,8,128]{0,3,2,1:T(8,128)(2,1)S(1)} %get-tuple-element.20), channel_id=1, source_target_pairs={{0,64},{64,128},{128,192},{1,65},{65,129},{129,193},{2,66},{66,130... | collective-permute-start | bytes 786440 | tf_op jit(solution)/shard_map/ppermute | solution.py:16
  205.8 8.5 %collective-permute-start.7 = (bf16[128,1,8,128]{0,3,2,1:T(8,128)(2,1)S(1)}, bf16[128,1,8,128]{0,3,2,1:T(8,128)(2,1)S(1)}, u32[]{:S(2)}, u32[]{:S(2)}) collective-permute-start(bf16[128,1,8,128]{0,3,2,1:T(8,128)(2,1)S(1)} %get-tuple-element.21), channel_id=1, source_target_pairs={{64,0},{128,64},{192,128},{65,1},{129,65},{193,129},{66,2},{130,66... | collective-permute-start | bytes 786440 | tf_op jit(solution)/shard_map/ppermute | solution.py:17
  214.4 11.8 %collective-permute-start.8 = (bf16[128,10,1,128]{0,3,2,1:T(8,128)(2,1)S(1)}, bf16[128,10,1,128]{0,3,2,1:T(8,128)(2,1)S(1)}, u32[]{:S(2)}, u32[]{:S(2)}) collective-permute-start(bf16[128,10,1,128]{0,3,2,1:T(8,128)(2,1)S(1)} %get-tuple-element.14), channel_id=1, source_target_pairs={{0,4},{4,8},{8,12},{12,16},{16,20},{20,24},{24,28},{28,32},{32,36}... | collective-permute-start | bytes 983048 | tf_op jit(solution)/shard_map/ppermute | solution.py:16
  217.2 15.5 %collective-permute-start.9 = (bf16[128,10,1,128]{0,3,2,1:T(8,128)(2,1)S(1)}, bf16[128,10,1,128]{0,3,2,1:T(8,128)(2,1)S(1)}, u32[]{:S(2)}, u32[]{:S(2)}) collective-permute-start(bf16[128,10,1,128]{0,3,2,1:T(8,128)(2,1)S(1)} %get-tuple-element.15), channel_id=1, source_target_pairs={{4,0},{8,4},{12,8},{16,12},{20,16},{24,20},{28,24},{32,28},{36,32}... | collective-permute-start | bytes 983048 | tf_op jit(solution)/shard_map/ppermute | solution.py:17
  232.8 11.9 %collective-permute-start.10 = (bf16[128,10,10,1]{0,3,2,1:T(2,128)(2,1)S(1)}, bf16[128,10,10,1]{0,3,2,1:T(2,128)(2,1)S(1)}, u32[]{:S(2)}, u32[]{:S(2)}) collective-permute-start(bf16[128,10,10,1]{0,3,2,1:T(2,128)(2,1)S(1)} %get-tuple-element.8), channel_id=1, source_target_pairs={{0,1},{1,2},{2,3},{4,5},{5,6},{6,7},{8,9},{9,10},{10,11},{12,13},{... | collective-permute-start | bytes 76808 | tf_op jit(solution)/shard_map/ppermute | solution.py:16
  242.5 12.6 %copy-start = (f32[128,8,8,128]{0,3,2,1:T(8,128)S(1)}, f32[128,8,8,128]{0,3,2,1:T(8,128)}, u32[]{:S(2)}) copy-start(f32[128,8,8,128]{0,3,2,1:T(8,128)} %get-tuple-element.25) | copy-start | bytes 12582916
  242.5 9.6 %collective-permute-start.11 = (bf16[128,10,10,1]{0,3,2,1:T(2,128)(2,1)S(1)}, bf16[128,10,10,1]{0,3,2,1:T(2,128)(2,1)S(1)}, u32[]{:S(2)}, u32[]{:S(2)}) collective-permute-start(bf16[128,10,10,1]{0,3,2,1:T(2,128)(2,1)S(1)} %get-tuple-element.9), channel_id=1, source_target_pairs={{1,0},{2,1},{3,2},{5,4},{6,5},{7,6},{9,8},{10,9},{11,10},{13,12},{... | collective-permute-start | bytes 76808 | tf_op jit(solution)/shard_map/ppermute | solution.py:17
  259.7 6.4 %collective-permute-start.12 = (bf16[128,1,8,128]{0,3,2,1:T(8,128)(2,1)S(1)}, bf16[128,1,8,128]{0,3,2,1:T(8,128)(2,1)S(1)}, u32[]{:S(2)}, u32[]{:S(2)}) collective-permute-start(bf16[128,1,8,128]{0,3,2,1:T(8,128)(2,1)S(1)} %get-tuple-element.18), channel_id=1, source_target_pairs={{0,64},{64,128},{128,192},{1,65},{65,129},{129,193},{2,66},{66,130... | collective-permute-start | bytes 786440 | tf_op jit(solution)/shard_map/ppermute | solution.py:16
  262.8 7.1 %collective-permute-start.13 = (bf16[128,1,8,128]{0,3,2,1:T(8,128)(2,1)S(1)}, bf16[128,1,8,128]{0,3,2,1:T(8,128)(2,1)S(1)}, u32[]{:S(2)}, u32[]{:S(2)}) collective-permute-start(bf16[128,1,8,128]{0,3,2,1:T(8,128)(2,1)S(1)} %get-tuple-element.19), channel_id=1, source_target_pairs={{64,0},{128,64},{192,128},{65,1},{129,65},{193,129},{66,2},{130,66... | collective-permute-start | bytes 786440 | tf_op jit(solution)/shard_map/ppermute | solution.py:17
  270.0 13.4 %collective-permute-start.14 = (bf16[128,10,1,128]{0,3,2,1:T(8,128)(2,1)S(1)}, bf16[128,10,1,128]{0,3,2,1:T(8,128)(2,1)S(1)}, u32[]{:S(2)}, u32[]{:S(2)}) collective-permute-start(bf16[128,10,1,128]{0,3,2,1:T(8,128)(2,1)S(1)} %get-tuple-element.12), channel_id=1, source_target_pairs={{0,4},{4,8},{8,12},{12,16},{16,20},{20,24},{24,28},{28,32},{32,36}... | collective-permute-start | bytes 983048 | tf_op jit(solution)/shard_map/ppermute | solution.py:16
  274.5 13.4 %collective-permute-start.15 = (bf16[128,10,1,128]{0,3,2,1:T(8,128)(2,1)S(1)}, bf16[128,10,1,128]{0,3,2,1:T(8,128)(2,1)S(1)}, u32[]{:S(2)}, u32[]{:S(2)}) collective-permute-start(bf16[128,10,1,128]{0,3,2,1:T(8,128)(2,1)S(1)} %get-tuple-element.13), channel_id=1, source_target_pairs={{4,0},{8,4},{12,8},{16,12},{20,16},{24,20},{28,24},{32,28},{36,32}... | collective-permute-start | bytes 983048 | tf_op jit(solution)/shard_map/ppermute | solution.py:17
  288.0 4.3 %collective-permute-start.16 = (bf16[128,10,10,1]{0,3,2,1:T(2,128)(2,1)S(1)}, bf16[128,10,10,1]{0,3,2,1:T(2,128)(2,1)S(1)}, u32[]{:S(2)}, u32[]{:S(2)}) collective-permute-start(bf16[128,10,10,1]{0,3,2,1:T(2,128)(2,1)S(1)} %get-tuple-element.6), channel_id=1, source_target_pairs={{0,1},{1,2},{2,3},{4,5},{5,6},{6,7},{8,9},{9,10},{10,11},{12,13},{... | collective-permute-start | bytes 76808 | tf_op jit(solution)/shard_map/ppermute | solution.py:16
  289.9 9.3 %collective-permute-start.17 = (bf16[128,10,10,1]{0,3,2,1:T(2,128)(2,1)S(1)}, bf16[128,10,10,1]{0,3,2,1:T(2,128)(2,1)S(1)}, u32[]{:S(2)}, u32[]{:S(2)}) collective-permute-start(bf16[128,10,10,1]{0,3,2,1:T(2,128)(2,1)S(1)} %get-tuple-element.7), channel_id=1, source_target_pairs={{1,0},{2,1},{3,2},{5,4},{6,5},{7,6},{9,8},{10,9},{11,10},{13,12},{... | collective-permute-start | bytes 76808 | tf_op jit(solution)/shard_map/ppermute | solution.py:17
Sparse Core Ops, SparseCore 0:
  15.7 81.6 all-gather.1
  104.2 57.4 reduce-scatter.1
where the time goes:
time: 317 us; the launch traced here: 316 us
  waiting for transfers between devices  157 us (50%)
  starting transfers between devices  81.2 us (26%)
  matrix products  28.9 us (9%)
  other arithmetic  22.3 us (7%)
  between operations  14.3 us (5%)
  local copies, waits for them, and re-layouts  12.4 us (4%)
    reduce_scatter x1, waiting for transfers between devices, per_device(): lax.psum_scatter(partial_flux, 'col', scatter_dimension=1, tiled=True)  53.4 us
    ppermute x9, waiting for transfers between devices, padded_2(): after = lax.ppermute(first, axis, down)  42 us
    ppermute x9, starting transfers between devices, padded_2(): before = lax.ppermute(last, axis, up)  40.6 us
    all_gather x1, waiting for transfers between devices, per_device(): lax.all_gather(trace_values, ('row', 'gz'), axis=1, tiled=True)  32.9 us
    ppermute x9, waiting for transfers between devices, padded_2(): before = lax.ppermute(last, axis, up)  26.7 us
    ppermute x9, starting transfers between devices, padded_2(): after = lax.ppermute(first, axis, down)  23.4 us
    all_to_all x1, starting transfers between devices, per_device(): lax.all_to_all(surface_flux, 'gz', split_axis=1, concat_axis=0, tiled=True)  17.1 us
    dot_general x1, matrix products, per_device(): jnp.dot(owned_flux, placer, precision=lax.Precision.HIGHEST, preferred_el...  14 us
  transfers between devices with their start and end apart: 21, of which 17 were waited for; matrix products, arithmetic and copies ran while one was open for 7% of the time, Pallas kernels for 0%

commit v1 on v0

--- a/solution.py
+++ b/solution.py
@@ -46,7 +46,12 @@
     )
     layer_index = lax.axis_index("gz")
     chosen = lax.dynamic_slice_in_dim(
-        lax.all_gather(trace_values, ("row", "gz"), axis=1, tiled=True),
+        jnp.concatenate(
+            lax.all_to_all(
+                jnp.stack([trace_values] * lax.axis_size(("row", "gz"))), ("row", "gz"), 0, 0
+            ),
+            axis=1,
+        ),
         layer_index * side_group,
         side_group,
         0,

time: 317 us -> 371 us (1.17)
  waiting for transfers between devices: 157 us -> 202 us
  starting transfers between devices: 81.2 us -> 88.1 us
    ppermute x9, waiting for transfers between devices: 26.7 us -> 90.9 us  [padded_2(): before = lax.ppermute(last, axis, up)]
    all_gather x1 -> x0, waiting for transfers between devices: 32.9 us -> none  [per_device(): lax.all_gather(trace_values, ('row', 'gz'), axis=1, tiled=True)]
    all_to_all x0 -> x1, starting transfers between devices: none -> 11.6 us  [per_device(): lax.all_to_all(jnp.stack([trace_values] * lax.axis_size(('row', 'gz'))),...]
    ppermute x9, waiting for transfers between devices: 42 us -> 49.1 us  [padded_2(): after = lax.ppermute(first, axis, down)]
    ppermute x9, starting transfers between devices: 40.6 us -> 34.3 us  [padded_2(): before = lax.ppermute(last, axis, up)]
    reduce_scatter x1, waiting for transfers between devices: 53.4 us -> 59.1 us  [per_device(): lax.psum_scatter(partial_flux, 'col', scatter_dimension=1, tiled=True)]
  transfers between devices with their start and end apart: 21 -> 21, of which waited for: 17 -> 16; matrix products, arithmetic and copies ran while one was open for 7% -> 6% of each run, Pallas kernels for 0% -> 0%
where the time goes in v1:
time: 371 us; the launch traced here: 370 us
  waiting for transfers between devices  202 us (54%)
  starting transfers between devices  88.1 us (24%)
  matrix products  28.1 us (8%)
  other arithmetic  22.4 us (6%)
  local copies, waits for them, and re-layouts  15.3 us (4%)
  between operations  14.3 us (4%)
    ppermute x9, waiting for transfers between devices, padded_2(): before = lax.ppermute(last, axis, up)  90.9 us
    reduce_scatter x1, waiting for transfers between devices, per_device(): lax.psum_scatter(partial_flux, 'col', scatter_dimension=1, tiled=True)  59.1 us
    ppermute x9, waiting for transfers between devices, padded_2(): after = lax.ppermute(first, axis, down)  49.1 us
    ppermute x9, starting transfers between devices, padded_2(): before = lax.ppermute(last, axis, up)  34.3 us
    ppermute x9, starting transfers between devices, padded_2(): after = lax.ppermute(first, axis, down)  25.1 us
    all_to_all x1, starting transfers between devices, per_device(): lax.all_to_all(surface_flux, 'gz', split_axis=1, concat_axis=0, tiled=True)  17.1 us
    dot_general x1, matrix products, per_device(): jnp.dot(owned_flux, placer, precision=lax.Precision.HIGHEST, preferred_el...  14 us
    unnamed x11, local copies, waits for them, and re-layouts  11.7 us
  transfers between devices with their start and end apart: 21, of which 16 were waited for; matrix products, arithmetic and copies ran while one was open for 6% of the time, Pallas kernels for 0%

profile of v1, /device:TPU:17, one launch (start us, length us, event | category | flops | bytes accessed | tf_op | source)
XLA Modules:
  0.0 369.8 jit_solution(977284615711343569)
XLA Ops:
  7.2 6.3 %fusion.28 = bf16[128,1024]{0,1:T(8,128)(2,1)S(1)} fusion(bf16[16,8,64,128]{3,2,1,0:T(8,128)(2,1)} %bitcast.30, s32[1024]{0:T(1024)} %bitcast.32), kind=kOutput, calls=%fused_computation.49 | convolution fusion | flops 2164391936 | bytes 2363392 | tf_op jit(solution)/shard_map/dot_general | solution.py:44
  13.5 2.8 stack.2
  16.3 11.6 %all-to-all-start = ((bf16[16,128,1024]{1,2,0:T(8,128)(2,1)}), bf16[16,128,1024]{1,2,0:T(8,128)(2,1)}, u32[]{:S(2)}, u32[]{:S(2)}) async-start(bf16[16,128,1024]{1,2,0:T(8,128)(2,1)} %stack.2), calls=%async_computation | async-start | bytes 8388608 | tf_op jit(solution)/shard_map/all_to_all | solution.py:50
  27.9 0.0 reduce-scatter.2.cloned.1.call-start
  28.0 3.3 copy.16
  31.4 3.3 collective-permute-start
  34.6 1.3 collective-permute-start.1
  35.9 39.0 %collective-permute-done = bf16[128,1,8,128]{0,3,2,1:T(8,128)(2,1)S(1)} collective-permute-done((bf16[128,1,8,128]{0,3,2,1:T(8,128)(2,1)S(1)}, bf16[128,1,8,128]{0,3,2,1:T(8,128)(2,1)S(1)}, u32[]{:S(2)}, u32[]{:S(2)}) %collective-permute-start) | collective-permute-done | bytes 262176 | tf_op jit(solution)/shard_map/ppermute | solution.py:16
  74.9 6.0 %collective-permute-done.1 = bf16[128,1,8,128]{0,3,2,1:T(8,128)(2,1)S(1)} collective-permute-done((bf16[128,1,8,128]{0,3,2,1:T(8,128)(2,1)S(1)}, bf16[128,1,8,128]{0,3,2,1:T(8,128)(2,1)S(1)}, u32[]{:S(2)}, u32[]{:S(2)}) %collective-permute-start.1) | collective-permute-done | bytes 262176 | tf_op jit(solution)/shard_map/ppermute | solution.py:17
  80.9 1.0 pad_maximum_fusion.8
  81.9 1.9 collective-permute-start.2
  83.8 6.1 %collective-permute-start.3 = (bf16[128,10,1,128]{0,3,2,1:T(8,128)(2,1)}, bf16[128,10,1,128]{0,3,2,1:T(8,128)(2,1)S(1)}, u32[]{:S(2)}, u32[]{:S(2)}) collective-permute-start(bf16[128,10,1,128]{0,3,2,1:T(8,128)(2,1)} %get-tuple-element.17), channel_id=1, source_target_pairs={{4,0},{8,4},{12,8},{16,12},{20,16},{24,20},{28,24},{32,28},{36,32}... | collective-permute-start | bytes 983048 | tf_op jit(solution)/shard_map/ppermute | solution.py:17
  89.9 36.6 %collective-permute-done.2 = bf16[128,10,1,128]{0,3,2,1:T(8,128)(2,1)S(1)} collective-permute-done((bf16[128,10,1,128]{0,3,2,1:T(8,128)(2,1)}, bf16[128,10,1,128]{0,3,2,1:T(8,128)(2,1)S(1)}, u32[]{:S(2)}, u32[]{:S(2)}) %collective-permute-start.2) | collective-permute-done | bytes 327712 | tf_op jit(solution)/shard_map/ppermute | solution.py:16
  126.5 9.2 %collective-permute-done.3 = bf16[128,10,1,128]{0,3,2,1:T(8,128)(2,1)S(1)} collective-permute-done((bf16[128,10,1,128]{0,3,2,1:T(8,128)(2,1)}, bf16[128,10,1,128]{0,3,2,1:T(8,128)(2,1)S(1)}, u32[]{:S(2)}, u32[]{:S(2)}) %collective-permute-start.3) | collective-permute-done | bytes 327712 | tf_op jit(solution)/shard_map/ppermute | solution.py:17
  135.7 0.1 pad_maximum_fusion.23
  135.7 6.1 %collective-permute-start.4 = (bf16[128,10,10,1]{0,3,2,1:T(2,128)(2,1)S(1)}, bf16[128,10,10,1]{0,3,2,1:T(2,128)(2,1)S(1)}, u32[]{:S(2)}, u32[]{:S(2)}) collective-permute-start(bf16[128,10,10,1]{0,3,2,1:T(2,128)(2,1)S(1)} %get-tuple-element.10), channel_id=1, source_target_pairs={{0,1},{1,2},{2,3},{4,5},{5,6},{6,7},{8,9},{9,10},{10,11},{12,13},{... | collective-permute-start | bytes 76808 | tf_op jit(solution)/shard_map/ppermute | solution.py:16
  141.9 1.9 collective-permute-start.5
  143.8 0.0 all-to-all-done
  143.8 7.7 %fusion.16 = f32[32,256]{0,1:T(8,128)} fusion(bf16[256,16384]{1,0:T(8,128)(2,1)} %param.9, bf16[128,16384]{0,1:T(8,128)(2,1)} %bitcast.3, s32[]{:T(128)S(6)} %select_n.3), kind=kOutput, calls=%fused_computation.37 | convolution fusion | flops 268435456 | bytes 12615684 | tf_op jit(solution)/shard_map/dot_general | solution.py:59
  151.6 0.0 reduce-scatter.2.cloned.1.call-update
  151.6 4.2 %copy.17 = bf16[128,8,8,128]{0,3,2,1:T(8,128)(2,1)} copy(bf16[128,8,8,128]{3,2,1,0:T(8,128)(2,1)} %param.7) | data formatting | bytes 4194304 | tf_op args[1]
  155.8 59.1 %reduce-scatter.2.cloned.1.call-done = f32[32,16]{0,1:T(8,128)} async-done(((f32[32,256]{0,1:T(8,128)}), f32[32,16]{0,1:T(8,128)}) %reduce-scatter.2.cloned.1.call-update) | async-done | bytes 2064 | tf_op jit(solution)/shard_map/reduce_scatter | solution.py:62
  214.9 1.4 reshape.51
  216.3 17.1 %all-to-all-start.1 = ((f32[4,1,128]{2,1,0:T(1,128)}), f32[4,1,128]{2,1,0:T(1,128)}, u32[]{:S(2)}, u32[]{:S(2)}) async-start(f32[4,1,128]{2,1,0:T(1,128)} %reshape.51), calls=%async_computation.2 | async-start | bytes 4096 | tf_op jit(solution)/shard_map/all_to_all | solution.py:63
  233.4 0.0 collective-permute-done.4
  233.4 0.0 collective-permute-done.5
  233.4 4.7 %maximum_convert_fusion = f32[128,10,10,130]{0,3,2,1:T(8,128)} fusion(bf16[128,10,10,1]{0,3,2,1:T(2,128)(2,1)S(1)} %collective-permute-done.5, bf16[128,10,1,128]{0,3,2,1:T(8,128)(2,1)S(1)} %collective-permute-done.3, bf16[128,1,8,128]{0,3,2,1:T(8,128)(2,1)S(1)} %collective-permute-done.1, bf16[128,8,8,128]{0,3,2,1:T(8,128)(2,1)S(1)} %copy.16, ...), kind=kLoop, calls=%fused_computation.43 | loop fusion | flops 23296000 | bytes 9984000 | tf_op jit(solution)/shard_map/convert_element_type | solution.py:23
  238.1 2.3 all-to-all-done.1
  240.5 0.5 broadcast.34
  241.0 1.3 reduce
  242.3 0.1 reshape.52
  242.4 0.1 reshape.49
  242.5 14.0 %fusion.18 = (bf16[128,8,8,128]{0,3,2,1:T(8,128)(2,1)S(1)}, f32[128,8,8,128]{0,3,2,1:T(8,128)}) fusion(f32[128,10,10,130]{0,3,2,1:T(8,128)} %maximum_convert_fusion, bf16[128,8,8,128]{0,3,2,1:T(8,128)(2,1)S(1)} %copy.16, f32[8,8,128]{2,1,0:T(8,128)S(1)} %broadcast_add_fusion, s32[8,8,128]{2,1,0:T(8,128)S(1)} %multiply_add_fusion, s32[4]{0:T(128)S(1)} %bitcast.33, ...), kind=kOutput, calls=%fused_computation.40 | convolution fusion | flops 66093056 | bytes 35719184 | tf_op jit(solution)/shard_map/dot_general | solution.py:68
  256.6 3.1 collective-permute-start.6
  259.7 1.3 collective-permute-start.7
  261.0 3.8 %collective-permute-done.6 = bf16[128,1,8,128]{0,3,2,1:T(8,128)(2,1)S(1)} collective-permute-done((bf16[128,1,8,128]{0,3,2,1:T(8,128)(2,1)S(1)}, bf16[128,1,8,128]{0,3,2,1:T(8,128)(2,1)S(1)}, u32[]{:S(2)}, u32[]{:S(2)}) %collective-permute-start.6) | collective-permute-done | bytes 262176 | tf_op jit(solution)/shard_map/ppermute | solution.py:16
  264.8 3.8 %collective-permute-done.7 = bf16[128,1,8,128]{0,3,2,1:T(8,128)(2,1)S(1)} collective-permute-done((bf16[128,1,8,128]{0,3,2,1:T(8,128)(2,1)S(1)}, bf16[128,1,8,128]{0,3,2,1:T(8,128)(2,1)S(1)}, u32[]{:S(2)}, u32[]{:S(2)}) %collective-permute-start.7) | collective-permute-done | bytes 262176 | tf_op jit(solution)/shard_map/ppermute | solution.py:17
  268.6 0.1 pad_maximum_fusion.5
  268.7 2.8 collective-permute-start.8
  271.6 5.2 %collective-permute-start.9 = (bf16[128,10,1,128]{0,3,2,1:T(8,128)(2,1)S(1)}, bf16[128,10,1,128]{0,3,2,1:T(8,128)(2,1)S(1)}, u32[]{:S(2)}, u32[]{:S(2)}) collective-permute-start(bf16[128,10,1,128]{0,3,2,1:T(8,128)(2,1)S(1)} %get-tuple-element.15), channel_id=1, source_target_pairs={{4,0},{8,4},{12,8},{16,12},{20,16},{24,20},{28,24},{32,28},{36,32}... | collective-permute-start | bytes 983048 | tf_op jit(solution)/shard_map/ppermute | solution.py:17
  276.7 4.2 %collective-permute-done.8 = bf16[128,10,1,128]{0,3,2,1:T(8,128)(2,1)S(1)} collective-permute-done((bf16[128,10,1,128]{0,3,2,1:T(8,128)(2,1)S(1)}, bf16[128,10,1,128]{0,3,2,1:T(8,128)(2,1)S(1)}, u32[]{:S(2)}, u32[]{:S(2)}) %collective-permute-start.8) | collective-permute-done | bytes 327712 | tf_op jit(solution)/shard_map/ppermute | solution.py:16
  281.0 7.4 %collective-permute-done.9 = bf16[128,10,1,128]{0,3,2,1:T(8,128)(2,1)S(1)} collective-permute-done((bf16[128,10,1,128]{0,3,2,1:T(8,128)(2,1)S(1)}, bf16[128,10,1,128]{0,3,2,1:T(8,128)(2,1)S(1)}, u32[]{:S(2)}, u32[]{:S(2)}) %collective-permute-start.9) | collective-permute-done | bytes 327712 | tf_op jit(solution)/shard_map/ppermute | solution.py:17
  288.3 0.1 pad_maximum_fusion.18
  288.4 7.5 %collective-permute-start.10 = (bf16[128,10,10,1]{0,3,2,1:T(2,128)(2,1)S(1)}, bf16[128,10,10,1]{0,3,2,1:T(2,128)(2,1)S(1)}, u32[]{:S(2)}, u32[]{:S(2)}) collective-permute-start(bf16[128,10,10,1]{0,3,2,1:T(2,128)(2,1)S(1)} %get-tuple-element.8), channel_id=1, source_target_pairs={{0,1},{1,2},{2,3},{4,5},{5,6},{6,7},{8,9},{9,10},{10,11},{12,13},{... | collective-permute-start | bytes 76808 | tf_op jit(solution)/shard_map/ppermute | solution.py:16
  296.0 2.2 collective-permute-start.11
  298.2 7.4 %collective-permute-done.11 = bf16[128,10,10,1]{0,3,2,1:T(2,128)(2,1)S(1)} collective-permute-done((bf16[128,10,10,1]{0,3,2,1:T(2,128)(2,1)S(1)}, bf16[128,10,10,1]{0,3,2,1:T(2,128)(2,1)S(1)}, u32[]{:S(2)}, u32[]{:S(2)}) %collective-permute-start.11) | collective-permute-done | bytes 25632 | tf_op jit(solution)/shard_map/ppermute | solution.py:17
  305.6 3.0 maximum_convert_fusion.1
  308.5 4.5 %fusion.19 = bf16[128,8,8,128]{0,3,2,1:T(8,128)(2,1)S(1)} fusion(f32[128,8,8,128]{0,3,2,1:T(8,128)S(1)} %copy-done, f32[128,10,10,130]{0,3,2,1:T(8,128)S(1)} %maximum_convert_fusion.1, bf16[128,8,8,128]{0,3,2,1:T(8,128)(2,1)S(1)} %get-tuple-element.24, f32[8,8,128]{2,1,0:T(8,128)S(1)} %broadcast_add_fusion), kind=kLoop, calls=%fused_computation.41 | loop fusion | flops 13631488 | bytes 33587200 | tf_op jit(solution)/shard_map/convert_element_type | solution.py:28
  313.1 3.1 collective-permute-start.12
  316.3 1.3 collective-permute-start.13
  317.6 2.0 collective-permute-done.12
  319.5 3.8 %collective-permute-done.13 = bf16[128,1,8,128]{0,3,2,1:T(8,128)(2,1)S(1)} collective-permute-done((bf16[128,1,8,128]{0,3,2,1:T(8,128)(2,1)S(1)}, bf16[128,1,8,128]{0,3,2,1:T(8,128)(2,1)S(1)}, u32[]{:S(2)}, u32[]{:S(2)}) %collective-permute-start.13) | collective-permute-done | bytes 262176 | tf_op jit(solution)/shard_map/ppermute | solution.py:17
  323.4 0.1 pad_maximum_fusion.2
  323.5 4.5 %collective-permute-start.14 = (bf16[128,10,1,128]{0,3,2,1:T(8,128)(2,1)S(1)}, bf16[128,10,1,128]{0,3,2,1:T(8,128)(2,1)S(1)}, u32[]{:S(2)}, u32[]{:S(2)}) collective-permute-start(bf16[128,10,1,128]{0,3,2,1:T(8,128)(2,1)S(1)} %get-tuple-element.12), channel_id=1, source_target_pairs={{0,4},{4,8},{8,12},{12,16},{16,20},{20,24},{24,28},{28,32},{32,36}... | collective-permute-start | bytes 983048 | tf_op jit(solution)/shard_map/ppermute | solution.py:16
  328.0 3.5 collective-permute-start.15
  331.4 5.4 %collective-permute-done.14 = bf16[128,10,1,128]{0,3,2,1:T(8,128)(2,1)S(1)} collective-permute-done((bf16[128,10,1,128]{0,3,2,1:T(8,128)(2,1)S(1)}, bf16[128,10,1,128]{0,3,2,1:T(8,128)(2,1)S(1)}, u32[]{:S(2)}, u32[]{:S(2)}) %collective-permute-start.14) | collective-permute-done | bytes 327712 | tf_op jit(solution)/shard_map/ppermute | solution.py:16
  336.8 4.5 %collective-permute-done.15 = bf16[128,10,1,128]{0,3,2,1:T(8,128)(2,1)S(1)} collective-permute-done((bf16[128,10,1,128]{0,3,2,1:T(8,128)(2,1)S(1)}, bf16[128,10,1,128]{0,3,2,1:T(8,128)(2,1)S(1)}, u32[]{:S(2)}, u32[]{:S(2)}) %collective-permute-start.15) | collective-permute-done | bytes 327712 | tf_op jit(solution)/shard_map/ppermute | solution.py:17
  341.3 0.1 pad_maximum_fusion.13
  341.4 1.9 collective-permute-start.16
  343.3 2.4 collective-permute-start.17
  345.8 6.9 %collective-permute-done.17 = bf16[128,10,10,1]{0,3,2,1:T(2,128)(2,1)S(1)} collective-permute-done((bf16[128,10,10,1]{0,3,2,1:T(2,128)(2,1)S(1)}, bf16[128,10,10,1]{0,3,2,1:T(2,128)(2,1)S(1)}, u32[]{:S(2)}, u32[]{:S(2)}) %collective-permute-start.17) | collective-permute-done | bytes 25632 | tf_op jit(solution)/shard_map/ppermute | solution.py:17
  352.7 3.0 maximum_convert_fusion.2
  355.6 4.5 %fusion.20 = bf16[128,8,8,128]{0,3,2,1:T(8,128)(2,1)S(1)} fusion(f32[128,8,8,128]{0,3,2,1:T(8,128)S(1)} %copy-done, f32[128,10,10,130]{0,3,2,1:T(8,128)S(1)} %maximum_convert_fusion.2, bf16[128,8,8,128]{0,3,2,1:T(8,128)(2,1)S(1)} %fusion.19, f32[8,8,128]{2,1,0:T(8,128)S(1)} %broadcast_add_fusion), kind=kLoop, calls=%fused_computation.42 | loop fusion | flops 13631488 | bytes 33587200 | tf_op jit(solution)/shard_map/convert_element_type | solution.py:28
  360.2 2.8 copy.22
  (15 shorter events, 0.2 us)
Async XLA Ops:
  16.3 127.5 %all-to-all-start = ((bf16[16,128,1024]{1,2,0:T(8,128)(2,1)}), bf16[16,128,1024]{1,2,0:T(8,128)(2,1)}, u32[]{:S(2)}, u32[]{:S(2)}) async-start(bf16[16,128,1024]{1,2,0:T(8,128)(2,1)} %stack.2), calls=%async_computation | async-start | bytes 8388608 | tf_op jit(solution)/shard_map/all_to_all | solution.py:50
  27.9 61.9 %copy-start.1 = (f32[8,8,128]{2,1,0:T(8,128)S(1)}, f32[8,8,128]{2,1,0:T(8,128)}, u32[]{:S(2)}) copy-start(f32[8,8,128]{2,1,0:T(8,128)} %param.8) | copy-start | bytes 98308
  27.9 187.0 %reduce-scatter.2.cloned.1.call-start = ((), (), s32[]{:S(2)}) async-start(), calls=%async_computation.3 | async-start | bytes 139264 | tf_op jit(solution)/shard_map/reduce_scatter | solution.py:62
  31.4 43.6 %collective-permute-start = (bf16[128,1,8,128]{0,3,2,1:T(8,128)(2,1)S(1)}, bf16[128,1,8,128]{0,3,2,1:T(8,128)(2,1)S(1)}, u32[]{:S(2)}, u32[]{:S(2)}) collective-permute-start(bf16[128,1,8,128]{0,3,2,1:T(8,128)(2,1)S(1)} %get-tuple-element.22), channel_id=1, source_target_pairs={{0,64},{64,128},{128,192},{1,65},{65,129},{129,193},{2,66},{66,130... | collective-permute-start | bytes 786440 | tf_op jit(solution)/shard_map/ppermute | solution.py:16
  34.6 46.3 %collective-permute-start.1 = (bf16[128,1,8,128]{0,3,2,1:T(8,128)(2,1)S(1)}, bf16[128,1,8,128]{0,3,2,1:T(8,128)(2,1)S(1)}, u32[]{:S(2)}, u32[]{:S(2)}) collective-permute-start(bf16[128,1,8,128]{0,3,2,1:T(8,128)(2,1)S(1)} %get-tuple-element.23), channel_id=1, source_target_pairs={{64,0},{128,64},{192,128},{65,1},{129,65},{193,129},{66,2},{130,66... | collective-permute-start | bytes 786440 | tf_op jit(solution)/shard_map/ppermute | solution.py:17
  81.9 44.6 %collective-permute-start.2 = (bf16[128,10,1,128]{0,3,2,1:T(8,128)(2,1)}, bf16[128,10,1,128]{0,3,2,1:T(8,128)(2,1)S(1)}, u32[]{:S(2)}, u32[]{:S(2)}) collective-permute-start(bf16[128,10,1,128]{0,3,2,1:T(8,128)(2,1)} %get-tuple-element.16), channel_id=1, source_target_pairs={{0,4},{4,8},{8,12},{12,16},{16,20},{20,24},{24,28},{28,32},{32,36}... | collective-permute-start | bytes 983048 | tf_op jit(solution)/shard_map/ppermute | solution.py:16
  83.8 51.9 %collective-permute-start.3 = (bf16[128,10,1,128]{0,3,2,1:T(8,128)(2,1)}, bf16[128,10,1,128]{0,3,2,1:T(8,128)(2,1)S(1)}, u32[]{:S(2)}, u32[]{:S(2)}) collective-permute-start(bf16[128,10,1,128]{0,3,2,1:T(8,128)(2,1)} %get-tuple-element.17), channel_id=1, source_target_pairs={{4,0},{8,4},{12,8},{16,12},{20,16},{24,20},{28,24},{32,28},{36,32}... | collective-permute-start | bytes 983048 | tf_op jit(solution)/shard_map/ppermute | solution.py:17
  135.7 97.6 %collective-permute-start.4 = (bf16[128,10,10,1]{0,3,2,1:T(2,128)(2,1)S(1)}, bf16[128,10,10,1]{0,3,2,1:T(2,128)(2,1)S(1)}, u32[]{:S(2)}, u32[]{:S(2)}) collective-permute-start(bf16[128,10,10,1]{0,3,2,1:T(2,128)(2,1)S(1)} %get-tuple-element.10), channel_id=1, source_target_pairs={{0,1},{1,2},{2,3},{4,5},{5,6},{6,7},{8,9},{9,10},{10,11},{12,13},{... | collective-permute-start | bytes 76808 | tf_op jit(solution)/shard_map/ppermute | solution.py:16
  141.9 91.5 %collective-permute-start.5 = (bf16[128,10,10,1]{0,3,2,1:T(2,128)(2,1)S(1)}, bf16[128,10,10,1]{0,3,2,1:T(2,128)(2,1)S(1)}, u32[]{:S(2)}, u32[]{:S(2)}) collective-permute-start(bf16[128,10,10,1]{0,3,2,1:T(2,128)(2,1)S(1)} %get-tuple-element.11), channel_id=1, source_target_pairs={{1,0},{2,1},{3,2},{5,4},{6,5},{7,6},{9,8},{10,9},{11,10},{13,12},{... | collective-permute-start | bytes 76808 | tf_op jit(solution)/shard_map/ppermute | solution.py:17
  216.3 24.2 %all-to-all-start.1 = ((f32[4,1,128]{2,1,0:T(1,128)}), f32[4,1,128]{2,1,0:T(1,128)}, u32[]{:S(2)}, u32[]{:S(2)}) async-start(f32[4,1,128]{2,1,0:T(1,128)} %reshape.51), calls=%async_computation.2 | async-start | bytes 4096 | tf_op jit(solution)/shard_map/all_to_all | solution.py:63
  233.4 9.1 %copy-start.2 = (s32[1,1,1,4]{3,2,1,0:T(1,128)S(1)}, s32[1,1,1,4]{3,2,1,0:T(1,128)}, u32[]{:S(2)}) copy-start(s32[1,1,1,4]{3,2,1,0:T(1,128)} %param.11) | copy-start | bytes 52
  256.6 8.2 %collective-permute-start.6 = (bf16[128,1,8,128]{0,3,2,1:T(8,128)(2,1)S(1)}, bf16[128,1,8,128]{0,3,2,1:T(8,128)(2,1)S(1)}, u32[]{:S(2)}, u32[]{:S(2)}) collective-permute-start(bf16[128,1,8,128]{0,3,2,1:T(8,128)(2,1)S(1)} %get-tuple-element.20), channel_id=1, source_target_pairs={{0,64},{64,128},{128,192},{1,65},{65,129},{129,193},{2,66},{66,130... | collective-permute-start | bytes 786440 | tf_op jit(solution)/shard_map/ppermute | solution.py:16
  259.7 8.9 %collective-permute-start.7 = (bf16[128,1,8,128]{0,3,2,1:T(8,128)(2,1)S(1)}, bf16[128,1,8,128]{0,3,2,1:T(8,128)(2,1)S(1)}, u32[]{:S(2)}, u32[]{:S(2)}) collective-permute-start(bf16[128,1,8,128]{0,3,2,1:T(8,128)(2,1)S(1)} %get-tuple-element.21), channel_id=1, source_target_pairs={{64,0},{128,64},{192,128},{65,1},{129,65},{193,129},{66,2},{130,66... | collective-permute-start | bytes 786440 | tf_op jit(solution)/shard_map/ppermute | solution.py:17
  268.7 12.2 %collective-permute-start.8 = (bf16[128,10,1,128]{0,3,2,1:T(8,128)(2,1)S(1)}, bf16[128,10,1,128]{0,3,2,1:T(8,128)(2,1)S(1)}, u32[]{:S(2)}, u32[]{:S(2)}) collective-permute-start(bf16[128,10,1,128]{0,3,2,1:T(8,128)(2,1)S(1)} %get-tuple-element.14), channel_id=1, source_target_pairs={{0,4},{4,8},{8,12},{12,16},{16,20},{20,24},{24,28},{28,32},{32,36}... | collective-permute-start | bytes 983048 | tf_op jit(solution)/shard_map/ppermute | solution.py:16
  271.6 16.8 %collective-permute-start.9 = (bf16[128,10,1,128]{0,3,2,1:T(8,128)(2,1)S(1)}, bf16[128,10,1,128]{0,3,2,1:T(8,128)(2,1)S(1)}, u32[]{:S(2)}, u32[]{:S(2)}) collective-permute-start(bf16[128,10,1,128]{0,3,2,1:T(8,128)(2,1)S(1)} %get-tuple-element.15), channel_id=1, source_target_pairs={{4,0},{8,4},{12,8},{16,12},{20,16},{24,20},{28,24},{32,28},{36,32}... | collective-permute-start | bytes 983048 | tf_op jit(solution)/shard_map/ppermute | solution.py:17
  288.4 9.7 %collective-permute-start.10 = (bf16[128,10,10,1]{0,3,2,1:T(2,128)(2,1)S(1)}, bf16[128,10,10,1]{0,3,2,1:T(2,128)(2,1)S(1)}, u32[]{:S(2)}, u32[]{:S(2)}) collective-permute-start(bf16[128,10,10,1]{0,3,2,1:T(2,128)(2,1)S(1)} %get-tuple-element.8), channel_id=1, source_target_pairs={{0,1},{1,2},{2,3},{4,5},{5,6},{6,7},{8,9},{9,10},{10,11},{12,13},{... | collective-permute-start | bytes 76808 | tf_op jit(solution)/shard_map/ppermute | solution.py:16
  295.9 12.6 %copy-start = (f32[128,8,8,128]{0,3,2,1:T(8,128)S(1)}, f32[128,8,8,128]{0,3,2,1:T(8,128)}, u32[]{:S(2)}) copy-start(f32[128,8,8,128]{0,3,2,1:T(8,128)} %get-tuple-element.25) | copy-start | bytes 12582916
  296.0 9.6 %collective-permute-start.11 = (bf16[128,10,10,1]{0,3,2,1:T(2,128)(2,1)S(1)}, bf16[128,10,10,1]{0,3,2,1:T(2,128)(2,1)S(1)}, u32[]{:S(2)}, u32[]{:S(2)}) collective-permute-start(bf16[128,10,10,1]{0,3,2,1:T(2,128)(2,1)S(1)} %get-tuple-element.9), channel_id=1, source_target_pairs={{1,0},{2,1},{3,2},{5,4},{6,5},{7,6},{9,8},{10,9},{11,10},{13,12},{... | collective-permute-start | bytes 76808 | tf_op jit(solution)/shard_map/ppermute | solution.py:17
  313.1 6.4 %collective-permute-start.12 = (bf16[128,1,8,128]{0,3,2,1:T(8,128)(2,1)S(1)}, bf16[128,1,8,128]{0,3,2,1:T(8,128)(2,1)S(1)}, u32[]{:S(2)}, u32[]{:S(2)}) collective-permute-start(bf16[128,1,8,128]{0,3,2,1:T(8,128)(2,1)S(1)} %get-tuple-element.18), channel_id=1, source_target_pairs={{0,64},{64,128},{128,192},{1,65},{65,129},{129,193},{2,66},{66,130... | collective-permute-start | bytes 786440 | tf_op jit(solution)/shard_map/ppermute | solution.py:16
  316.3 7.1 %collective-permute-start.13 = (bf16[128,1,8,128]{0,3,2,1:T(8,128)(2,1)S(1)}, bf16[128,1,8,128]{0,3,2,1:T(8,128)(2,1)S(1)}, u32[]{:S(2)}, u32[]{:S(2)}) collective-permute-start(bf16[128,1,8,128]{0,3,2,1:T(8,128)(2,1)S(1)} %get-tuple-element.19), channel_id=1, source_target_pairs={{64,0},{128,64},{192,128},{65,1},{129,65},{193,129},{66,2},{130,66... | collective-permute-start | bytes 786440 | tf_op jit(solution)/shard_map/ppermute | solution.py:17
  323.5 13.4 %collective-permute-start.14 = (bf16[128,10,1,128]{0,3,2,1:T(8,128)(2,1)S(1)}, bf16[128,10,1,128]{0,3,2,1:T(8,128)(2,1)S(1)}, u32[]{:S(2)}, u32[]{:S(2)}) collective-permute-start(bf16[128,10,1,128]{0,3,2,1:T(8,128)(2,1)S(1)} %get-tuple-element.12), channel_id=1, source_target_pairs={{0,4},{4,8},{8,12},{12,16},{16,20},{20,24},{24,28},{28,32},{32,36}... | collective-permute-start | bytes 983048 | tf_op jit(solution)/shard_map/ppermute | solution.py:16
  328.0 13.4 %collective-permute-start.15 = (bf16[128,10,1,128]{0,3,2,1:T(8,128)(2,1)S(1)}, bf16[128,10,1,128]{0,3,2,1:T(8,128)(2,1)S(1)}, u32[]{:S(2)}, u32[]{:S(2)}) collective-permute-start(bf16[128,10,1,128]{0,3,2,1:T(8,128)(2,1)S(1)} %get-tuple-element.13), channel_id=1, source_target_pairs={{4,0},{8,4},{12,8},{16,12},{20,16},{24,20},{28,24},{32,28},{36,32}... | collective-permute-start | bytes 983048 | tf_op jit(solution)/shard_map/ppermute | solution.py:17
  341.4 4.3 %collective-permute-start.16 = (bf16[128,10,10,1]{0,3,2,1:T(2,128)(2,1)S(1)}, bf16[128,10,10,1]{0,3,2,1:T(2,128)(2,1)S(1)}, u32[]{:S(2)}, u32[]{:S(2)}) collective-permute-start(bf16[128,10,10,1]{0,3,2,1:T(2,128)(2,1)S(1)} %get-tuple-element.6), channel_id=1, source_target_pairs={{0,1},{1,2},{2,3},{4,5},{5,6},{6,7},{8,9},{9,10},{10,11},{12,13},{... | collective-permute-start | bytes 76808 | tf_op jit(solution)/shard_map/ppermute | solution.py:16
  343.3 9.3 %collective-permute-start.17 = (bf16[128,10,10,1]{0,3,2,1:T(2,128)(2,1)S(1)}, bf16[128,10,10,1]{0,3,2,1:T(2,128)(2,1)S(1)}, u32[]{:S(2)}, u32[]{:S(2)}) collective-permute-start(bf16[128,10,10,1]{0,3,2,1:T(2,128)(2,1)S(1)} %get-tuple-element.7), channel_id=1, source_target_pairs={{1,0},{2,1},{3,2},{5,4},{6,5},{7,6},{9,8},{10,9},{11,10},{13,12},{... | collective-permute-start | bytes 76808 | tf_op jit(solution)/shard_map/ppermute | solution.py:17
Sparse Core Ops, SparseCore 0:
  151.7 63.1 reduce-scatter.1
